TPU v7x, 32 devices: a whole 2x2x4 slice. The times are simulated.
32 devices in a mesh: groups: 2 (over x), span: 8 (over z, y), head: 2 (over core).
Axes of the slice: x: 2, y: 2, z: 4, core: 2. Of those that a mesh axis runs over, the one named last changes fastest.
Arguments:
- span_states: bfloat16 [2048, 4096], P(('groups', 'span'), 'head'), parts along dimension 0, may hold values from -1.5 to 1.5
- span_queries: bfloat16 [2048, 2048], P(('groups', 'span'), 'head'), parts along dimension 0, may hold values from -1000 to 1000
- span_memory: bfloat16 [2048, 2, 896], P(('groups', 'span'), None, 'head'), parts along dimension 0, may hold values from -1000 to 1000
- passages: bfloat16 [16384, 896], P(('groups', 'span')), parts along dimension 0, may hold values from -1.5 to 1.5
- neighbours: int32 [32, 2], P(('groups', 'span')), parts along dimension 0, may hold values from 0 to 63, as said below
- enc_query_w: bfloat16 [896, 896], P(None, 'head'), may hold values from -0.1875 to 0.1875
- enc_out_w: bfloat16 [896, 896], P(None, 'head'), may hold values from -0.1875 to 0.1875
- kv_weight: bfloat16 [896, 2, 2048], P(None, None, ('head', 'span')), may hold values from -0.1875 to 0.1875
- out_weight: bfloat16 [2048, 4096], P('head', 'span'), may hold values from -0.125 to 0.125
Outputs:
- mixed_states: bfloat16 [2048, 4096], P(('groups', 'span'), 'head'), parts along dimension 0
There are 2 independent parts, one for each index of `groups`. A program takes and returns all parts, laid end to end along the dimension named above; an argument that names none is the same for every part. Nothing has to cross between parts.
Inputs may be any that keep to these rules, and one draw needn't show every extreme that they name: `neighbours`: passage p belongs to index p // 8 of the span axis. Among the spans of one index of the span axis, all 4 passages listed belong to distinct indices.
All inputs are finite; a program needn't handle non-finite values.
Results may differ from a plain program's by a relative error of at most 0.025.
Values may be sent and summed in bfloat16 or wider, within the bound.
A program may use at most 64 MiB of HBM per device.

v0:
```python
import functools
import math

import jax
import jax.numpy as jnp
from jax import lax
from jax.experimental import pallas as pl
from jax.experimental.pallas import tpu as pltpu
from jax.sharding import PartitionSpec as P

HD = 128
E = 896
EHD = 64
CT = 64
PT = 128
NB = 2
PS_DEV = 8
MESH = pl.DeviceIdType.MESH


epsilon = 1e-06


def rms_rows(values):
    return values * lax.rsqrt(jnp.mean(values * values, axis=-1, keepdims=True) + epsilon)


def softmax_rows(scores):
    top_score = jnp.max(scores, axis=-1, keepdims=True)
    raised = jnp.exp(scores - top_score)
    return raised / jnp.sum(raised, axis=-1, keepdims=True)


def ring_place(span, n):
    odd = span % 2
    return (1 - odd) * (span // 2) + odd * (n - 1 - span // 2)


def ring_span(place, n):
    back = place // (n // 2)
    return (1 - back) * (2 * place) + back * (2 * (n - 1 - place) + 1)


def remote(src, dst, send_sem, recv_sem, **where):
    return pltpu.make_async_remote_copy(
        src_ref=src, dst_ref=dst, send_sem=send_sem, recv_sem=recv_sem,
        device_id=where, device_id_type=MESH,
    )


class Ring:
    def __init__(self, n, own, slots, sems):
        me = lax.axis_index("span")
        self.n, self.own, self.slots, self.sems = n, own, slots, sems
        self.place = ring_place(me, n)
        self.targets = (ring_span((self.place + 1) % n, n), ring_span((self.place + n - 1) % n, n))
        self.steps = n // 2
        self.copies = {}

    def travels(self, t, side, k):
        return t < self.steps - 1 or k % 2 == side

    def block(self, t, side):
        n = self.n
        return ring_span((self.place + (n - t if side == 0 else t)) % n, n)

    def send(self, t, side, k):
        dst = self.slots(self.block(t, side))[k]
        copy = remote(
            self.own[k] if t == 0 else dst, dst,
            self.sems.at[0, side, t, k], self.sems.at[1, side, t, k], span=self.targets[side],
        )
        copy.start()
        self.copies[t, side, k] = copy

    def start(self):
        for k in range(len(self.own)):
            for side in range(2):
                if self.travels(0, side, k):
                    self.send(0, side, k)

    def advance(self, t, forward=None):
        for k in range(len(self.own)):
            for side in range(2):
                if self.travels(t, side, k):
                    self.copies[t, side, k].wait_recv()
                    if t + 1 < self.steps and self.travels(t + 1, side, k):
                        self.send(t + 1, side, k)
                    if forward is not None:
                        forward(t, side, k, self.block(t + 1, side))
        return [self.block(t + 1, side) for side in range(1 if t == self.steps - 1 else 2)]

    def finish(self):
        for copy in self.copies.values():
            copy.wait_send()


def weigh(scores, mask):
    scores = jnp.where(mask, scores, -jnp.inf)
    raised = jnp.exp(scores - jnp.max(scores, axis=-1, keepdims=True))
    return (raised * (1.0 / jnp.sum(raised, axis=-1, keepdims=True))).astype(jnp.bfloat16)


def same_span(shape, rows_each, lanes_each, spans):
    row = lax.broadcasted_iota(jnp.int32, shape, 0) // rows_each
    lane = (lax.broadcasted_iota(jnp.int32, shape, 1) // lanes_each) % spans
    return row == lane


def dot(a, b, dims=((1,), (0,))):
    return lax.dot_general(a, b, (dims, ((), ())), preferred_element_type=jnp.float32)


def greet_all(n):
    me = lax.axis_index("span")
    head = lax.axis_index("head")
    barrier = pltpu.get_barrier_semaphore()
    for d in range(n):
        for hop in range(2):
            if d or hop:
                pl.semaphore_signal(
                    barrier, inc=1,
                    device_id={"span": (me + d) % n, "head": (head + hop) % 2}, device_id_type=MESH,
                )
    return barrier, 2 * n - 1


def fetch_kernel(
    n, groups, spans, fused, nb_ref, pas_in, mem_ref, wq_ref, wo_ref, kv_ref, ask_in, w_in, states_in, *rest,
):
    if fused:
        (out_ref, enc, kvg, att_ref, *tail) = rest[:4 + 11]
        scratch = rest[4 + 11:]
    else:
        enc, kvg = rest[:2]
        scratch = rest[2:]
    (
        pas_ref, ask_ref, nb_own, nbg, nbs, picks, got, swap, cop, mem, wq, wo, query, mixed,
        local_sem, nb_sem, pas_sem, swap_sem, w_sem, enc_sem, ring_sem, twin_sem,
    ) = scratch
    me = lax.axis_index("span")
    head = lax.axis_index("head")
    group = lax.axis_index("groups")
    other = 1 - head
    twin = group + 1 - 2 * (group % 2)
    part = group % 2
    half_rows = PT // 2
    half_e = wq_ref.shape[0]
    barrier, greeted = greet_all(n)
    pl.semaphore_signal(barrier, inc=1, device_id={"groups": twin}, device_id_type=MESH)
    loads = [pltpu.make_async_copy(pas_in, pas_ref, local_sem.at[7])]
    if fused:
        loads += [
            pltpu.make_async_copy(ask_in, ask_ref, local_sem.at[8]),
            pltpu.make_async_copy(w_in, tail[0], local_sem.at[9]),
            pltpu.make_async_copy(states_in, tail[1], local_sem.at[10]),
        ]
    for copy in loads:
        copy.start()
    nb_own[...] = jnp.zeros_like(nb_own)
    nb_own[:spans, :NB] = nb_ref[...]
    pl.semaphore_wait(barrier, greeted + 1)

    nb_copies = []
    for d in range(1, n):
        copy = remote(nb_own, nbg.at[me], nb_sem.at[0, d], nb_sem.at[1, d], span=(me + d) % n)
        copy.start()
        nb_copies.append(copy)
    own_nb = pltpu.make_async_copy(nb_own, nbg.at[me], local_sem.at[0])
    own_nb.start()

    depth = kv_ref.shape[1]
    half, extra = depth // 2, depth // 28 * 3
    near, far = part, 1 - part

    def pieces(ref):
        return [
            ref.at[near, pl.ds(0, half)], ref.at[near, pl.ds(half, half)],
            ref.at[far, pl.ds(0, extra // 2)], ref.at[far, pl.ds(extra // 2, extra // 2)],
        ]

    ring = Ring(n, pieces(kv_ref), lambda block: pieces(kvg.at[block]), ring_sem)
    twins = [[] for _ in range(ring.steps)]

    def to_twin(t, side, k, block):
        if k < 2:
            lines = pl.ds(extra, half - extra) if k == 0 else pl.ds(half, half)
            piece = kvg.at[block, near, lines]
            copy = remote(piece, piece, twin_sem.at[0, side, t, k], twin_sem.at[1, side, t, k], groups=twin)
            copy.start()
            twins[t].append(copy)

    ring.start()
    mine = pl.ds(pl.multiple_of(head * half_e, half_e), half_e)
    w_copies, own_copies = [], []
    for i, (src, dst) in enumerate((
        (mem_ref.at[0], mem.at[0, mine]), (mem_ref.at[1], mem.at[1, mine]), (wq_ref, wq.at[mine]), (wo_ref, wo.at[mine]),
    )):
        w_copies.append(remote(src, dst, w_sem.at[0, i], w_sem.at[1, i], head=other))
        w_copies[-1].start()
        own_copies.append(pltpu.make_async_copy(src, dst, local_sem.at[3 + i]))
        own_copies[-1].start()
    own_copies.append(pltpu.make_async_copy(kv_ref, kvg.at[me], local_sem.at[1]))
    own_copies[-1].start()
    own_nb.wait()
    loads[0].wait()
    for copy in nb_copies:
        copy.wait()
    to_scalar = pltpu.make_async_copy(nbg, nbs, local_sem.at[2])
    to_scalar.start()
    to_scalar.wait()

    def pick(requester):
        index = jnp.int32(0)
        for e in range(spans * NB):
            wanted = nbs[requester, e // NB, e % NB]
            index = index + jnp.where(wanted // PS_DEV == me, wanted % PS_DEV, 0)
        return pas_ref[index, head]

    pas_copies = []
    picks[1] = pick((me + 1) % n)
    for d in range(1, n):
        if d + 1 < n:
            picks[d + 1] = pick((me + d + 1) % n)
        else:
            got[me] = pick(me)
        copy = remote(picks.at[d], got.at[me], pas_sem.at[0, d], pas_sem.at[1, d], span=(me + d) % n)
        copy.start()
        pas_copies.append(copy)

    arrivals = [ring.advance(0, to_twin)]
    for copy in pas_copies:
        copy.wait_recv()
    swaps = []
    for c in range(spans):
        swap[c] = got[nbs[me, c, other] // PS_DEV]
    for c in range(spans):
        spot = cop.at[pl.ds(pl.multiple_of(c * PT + head * half_rows, half_rows), half_rows)]
        copy = remote(swap.at[c], spot, swap_sem.at[0, c], swap_sem.at[1, c], head=other)
        copy.start()
        swaps.append(copy)
        spot[...] = got[nbs[me, c, head] // PS_DEV]
    for copy in own_copies:
        copy.wait()
    for copy in w_copies:
        copy.wait()
    for copy in swaps:
        copy.wait()

    arrivals.append(ring.advance(1, to_twin))
    rows = cop.shape[0]
    tokens = mem.shape[2]
    width = cop.shape[1]
    values = cop[...].astype(jnp.float32)
    query[...] = dot(rms_rows(values).astype(jnp.bfloat16), wq[...], ((1,), (1,))).astype(jnp.bfloat16)
    mask = same_span((rows, tokens), PT, CT, spans)
    feature = lax.broadcasted_iota(jnp.int32, (2 * EHD, tokens), 0) // EHD
    for j in range(width // (2 * EHD)):
        lines = pl.ds(j * 2 * EHD, 2 * EHD)
        total = None
        for e in range(2):
            keys = jnp.where(feature == e, mem[0, lines], jnp.bfloat16(0))
            vals = jnp.where(feature == e, mem[1, lines], jnp.bfloat16(0))
            scores = dot(query[:, lines], keys) * (1.0 / math.sqrt(EHD))
            term = dot(weigh(scores, mask), vals, ((1,), (1,)))
            total = term if e == 0 else total + term
        mixed[:, lines] = total.astype(jnp.bfloat16)
    branch = dot(mixed[...], wo[...])
    enc[head] = rms_rows(cop[...].astype(jnp.float32) + branch).astype(jnp.bfloat16)
    enc_copy = remote(enc.at[head], enc.at[head], enc_sem.at[0], enc_sem.at[1], head=other)
    enc_copy.start()
    if ring.steps > 2:
        arrivals.append(ring.advance(2, to_twin))
    enc_copy.wait_recv()

    if fused:
        loads[1].wait()
        asks = ask_ref.shape[0]
        dec_mask = same_span((asks, NB * rows), CT, PT, spans)

        def attend(block):
            for m in range(kv_ref.shape[2] // HD):
                flat = enc[...].reshape(NB * rows, width)
                lanes = pl.ds(m * HD, HD)
                keys = dot(flat, kvg[block, 0, :, lanes]).astype(jnp.bfloat16)
                vals = dot(flat, kvg[block, 1, :, lanes]).astype(jnp.bfloat16)
                spot = pl.ds(pl.multiple_of(block * kv_ref.shape[2] + m * HD, HD), HD)
                scores = dot(ask_ref[:, spot], keys, ((1,), (1,))) * (1.0 / math.sqrt(HD))
                att_ref[:, spot] = dot(weigh(scores, dec_mask), vals).astype(jnp.bfloat16)

        attend(me)

    for t in range(ring.steps):
        while len(arrivals) < min(t + 3, ring.steps):
            arrivals.append(ring.advance(len(arrivals), to_twin))
        for copy in twins[t]:
            copy.wait_recv()
        if fused:
            for block in arrivals[t]:
                attend(block)
    if fused:
        loads[2].wait()
        loads[3].wait()
        out_stage(n, att_ref, tail[0], tail[1], out_ref, *tail[2:])
    enc_copy.wait_send()
    for copy in pas_copies + [copy for pair in twins for copy in pair]:
        copy.wait_send()
    ring.finish()


def out_kernel(n, *refs):
    barrier, greeted = greet_all(n)
    pl.semaphore_wait(barrier, greeted)
    out_stage(n, *refs)


def out_stage(
    n, att_ref, w_ref, states_ref, out_ref,
    gathered, part, crossed, summed, back, ring_sem, cross_sem, send_sem, back_sem,
):
    me = lax.axis_index("span")
    head = lax.axis_index("head")
    other = 1 - head
    half = n // 2
    owner_head = me // half
    column = me % half
    rows = att_ref.shape[0]
    half_rows = rows // 2
    width = w_ref.shape[1]

    def pieces(ref):
        return [ref.at[pl.ds(k * half_rows, half_rows)] for k in range(2)]

    ring = Ring(n, pieces(att_ref), lambda block: pieces(gathered.at[block]), ring_sem)
    ring.start()
    crossings, returns = [], []

    def project(block, rows_ref):
        i = len(crossings)
        value = jnp.dot(rows_ref[...], w_ref[...], preferred_element_type=jnp.float32)
        value = value.astype(jnp.bfloat16)
        part[i, 0] = value[:half_rows]
        part[i, 1] = value[half_rows:]
        copy = remote(part.at[i, other], crossed.at[i], cross_sem.at[0, i], cross_sem.at[1, i], head=other)
        crossings.append((copy, block))

    def send_across():
        crossings[-1][0].start()

    def give_back():
        i = len(returns)
        copy, block = crossings[i]
        copy.wait_recv()
        total = part[i, head].astype(jnp.float32) + crossed[i].astype(jnp.float32)
        summed[i] = total.astype(jnp.bfloat16)
        copy = remote(
            summed.at[i], back.at[column, head], send_sem.at[i], back_sem.at[column, head],
            span=block, head=owner_head,
        )
        if i == 0:
            @pl.when(head != owner_head)
            def _():
                copy.start()

            @pl.when(head == owner_head)
            def _():
                back[column, head] = summed[i]
        else:
            copy.start()
        returns.append(copy)

    project(me, att_ref)
    send_across()
    for t in range(ring.steps):
        for block in ring.advance(t):
            project(block, gathered.at[block])
            send_across()
            give_back()
    give_back()

    for j in range(half):
        for source in range(2):
            mine = (head * half + j == me) & (head == source)

            @pl.when(jnp.logical_not(mine))
            def _():
                remote(
                    summed.at[0], back.at[j, source], send_sem.at[0], back_sem.at[j, source], head=other,
                ).wait_recv()

            lanes = pl.ds(j * width, width)
            lines = pl.ds(source * half_rows, half_rows)
            out_ref[lines, lanes] = (
                states_ref[lines, lanes].astype(jnp.float32) + back[j, source].astype(jnp.float32)
            ).astype(jnp.bfloat16)
    ring.finish()
    for copy, _ in crossings:
        copy.wait_send()
    for i, copy in enumerate(returns):
        if i == 0:
            @pl.when(head != owner_head)
            def _():
                copy.wait_send()
        else:
            copy.wait_send()


def call(kernel, collective_id, out_shape, scratch_shapes, spaces, *operands):
    return pl.pallas_call(
        kernel,
        out_shape=out_shape,
        in_specs=[pl.BlockSpec(memory_space=space) for space in spaces],
        out_specs=[pl.BlockSpec(memory_space=pltpu.VMEM)] * len(out_shape),
        scratch_shapes=scratch_shapes,
        compiler_params=pltpu.CompilerParams(collective_id=collective_id, has_side_effects=True),
    )(*operands)


def decode(encoded, kv_all, span_queries, span_count):
    dec_kv = jnp.einsum(
        "re,nsec->rsnc", encoded.reshape(-1, E), kv_all, preferred_element_type=jnp.float32
    ).astype(jnp.bfloat16)
    head_count = span_queries.shape[1] // HD
    dec_kv = dec_kv.reshape(NB, span_count, PT, 2, head_count, HD)
    dec_query = span_queries.reshape(span_count, CT, head_count, HD)
    scores = jnp.einsum(
        "cqhd,ncphd->chqnp", dec_query, dec_kv[:, :, :, 0], preferred_element_type=jnp.float32
    ) / math.sqrt(HD)
    scores = scores.reshape(span_count, head_count, CT, NB * PT)
    weights = softmax_rows(scores).astype(jnp.bfloat16)
    weights = weights.reshape(span_count, head_count, CT, NB, PT)
    attended = jnp.einsum(
        "chqnp,ncphd->cqhd", weights, dec_kv[:, :, :, 1], preferred_element_type=jnp.float32
    )
    return attended.astype(jnp.bfloat16).reshape(span_count * CT, head_count * HD)


def body(
    span_states,
    span_queries,
    span_memory,
    passages,
    neighbours,
    enc_query_w,
    enc_out_w,
    kv_weight,
    out_weight,
):
    n = lax.axis_size("span")
    span_count = neighbours.shape[0]
    bf16 = jnp.bfloat16
    dma = pltpu.SemaphoreType.DMA
    half_rows = PT // 2
    kv = kv_weight.transpose(1, 0, 2)
    memory = span_memory.transpose(1, 2, 0)
    rows, tokens = span_count * PT, span_memory.shape[0]
    sds = jax.ShapeDtypeStruct
    fused = kv.shape[2] % HD == 0
    enc_shape, kv_shape = (NB, rows, E), (n,) + kv.shape
    states, width = sds(span_states.shape, bf16), out_weight.shape[1]
    out_scratch = [
        pltpu.VMEM((n,) + span_queries.shape, bf16),
        pltpu.VMEM((n, 2, tokens // 2, width), bf16),
        pltpu.VMEM((n, tokens // 2, width), bf16),
        pltpu.VMEM((n, tokens // 2, width), bf16),
        pltpu.VMEM((n // 2, 2, tokens // 2, width), bf16),
        dma((2, 2, n // 2, 2)),
        dma((2, n)),
        dma((n,)),
        dma((n // 2, 2)),
    ]
    scratch = [
        pltpu.VMEM((passages.shape[0] // PT, 2, half_rows, E), bf16),
        pltpu.VMEM(span_queries.shape if fused else (16, 128), bf16),
        pltpu.VMEM((8, 128), jnp.int32),
        pltpu.VMEM((n, 8, 128), jnp.int32),
        pltpu.SMEM((n, 8, 128), jnp.int32),
        pltpu.VMEM((n, half_rows, E), bf16),
        pltpu.VMEM((n, half_rows, E), bf16),
        pltpu.VMEM((span_count, half_rows, E), bf16),
        pltpu.VMEM((rows, E), bf16),
        pltpu.VMEM((2, E, tokens), bf16),
        pltpu.VMEM((E, E), bf16),
        pltpu.VMEM((E, E), bf16),
        pltpu.VMEM((rows, E), bf16),
        pltpu.VMEM((rows, E), bf16),
        dma((11,)),
        dma((2, n)),
        dma((2, n)),
        dma((2, span_count)),
        dma((2, 4)),
        dma((2,)),
        dma((2, 2, n // 2, 4)),
        dma((2, 2, n // 2, 2)),
    ]
    if fused:
        scratch = [
            pltpu.VMEM(enc_shape, bf16), pltpu.VMEM(kv_shape, bf16), pltpu.VMEM(span_queries.shape, bf16),
            pltpu.VMEM(out_weight.shape, bf16), pltpu.VMEM(span_states.shape, bf16),
        ] + out_scratch + scratch
    found = call(
        functools.partial(fetch_kernel, n, lax.axis_size("groups"), span_count, fused), 0,
        [states] if fused else [sds(enc_shape, bf16), sds(kv_shape, bf16)],
        scratch, [pltpu.VMEM] + [pl.ANY] * 8,
        neighbours, passages.reshape(-1, 2, half_rows, E), memory, enc_query_w.T, enc_out_w.T, kv,
        span_queries, out_weight, span_states,
    )
    if fused:
        return found[0]
    attended = decode(found[0], found[1], span_queries, span_count)
    return call(
        functools.partial(out_kernel, n), 1, [states], out_scratch, [pltpu.VMEM] * 3,
        attended, out_weight, span_states,
    )[0]


def solution(mesh):
    placed = (
        P(("groups", "span"), "head"),
        P(("groups", "span"), "head"),
        P(("groups", "span"), None, "head"),
        P(("groups", "span"), None),
        P(("groups", "span"), None),
        P(None, "head"),
        P(None, "head"),
        P(None, None, ("head", "span")),
        P("head", "span"),
    )
    return jax.shard_map(
        body, mesh=mesh, in_specs=placed, out_specs=P(("groups", "span"), "head"), check_vma=False
    )
```

profile of v0, /device:TPU:1, one launch (start us, length us, event | category | flops | bytes accessed | tf_op | source)
XLA Modules:
  0.0 101.9 jit_solution(8257248579025533779)
XLA Ops:
  0.0 1.8 %copy.12 = bf16[896,2,128]{2,0,1:T(8,128)(2,1)} copy(bf16[896,2,128]{2,1,0:T(2,128)(2,1)} %param.16) | data formatting | bytes 917504 | tf_op args[7]
  1.8 98.1 %shard_map.91 = bf16[128,2048]{1,0:T(8,128)(2,1)} custom-call(s32[2,2]{1,0:T(2,128)} %nb_ref.1, bf16[8,2,64,896]{3,2,1,0:T(8,128)(2,1)} %bitcast.8, bf16[2,448,128]{2,1,0:T(8,128)(2,1)} %bitcast.11, bf16[448,896]{1,0:T(8,128)(2,1)} %bitcast.9, bf16[448,896]{1,0:T(8,128)(2,1)} %bitcast.10, bf16[2,896,128]{2,1,0:T(8,128)(2,1)} %bitcast.7, ...), custom_call_target="tpu_custom_call" | custom-call | tf_op jit(solution)/shard_map/pallas_call | solution.py:409
  100.0 1.9 %copy.14 = bf16[128,2048]{1,0:T(8,128)(2,1)} copy(bf16[128,2048]{1,0:T(8,128)(2,1)} %shard_map.91) | data formatting | bytes 1048576
where the time goes:
time: 102 us
  Pallas kernels  98.1 us (96%)
  local copies, waits for them, and re-layouts  3.73 us (4%)
    pallas_call x1, Pallas kernels, call(): pl.pallas_call(kernel, out_shape=out_shape, in_specs=[pl.BlockSpec(memory...  98.1 us
    unnamed x2, local copies, waits for them, and re-layouts  3.73 us

commit v1 on v0

--- a/solution.py
+++ b/solution.py
@@ -126,18 +126,10 @@
 
 
 def fetch_kernel(
-    n, groups, spans, fused, nb_ref, pas_in, mem_ref, wq_ref, wo_ref, kv_ref, ask_in, w_in, states_in, *rest,
+    n, spans, nb_ref, pas_in, mem_ref, wq_ref, wo_ref, kv_ref, enc, kvg,
+    pas_ref, nb_own, nbg, nbs, picks, got, swap, cop, mem, wq, wo, query, mixed,
+    local_sem, nb_sem, pas_sem, swap_sem, w_sem, enc_sem, ring_sem, twin_sem,
 ):
-    if fused:
-        (out_ref, enc, kvg, att_ref, *tail) = rest[:4 + 11]
-        scratch = rest[4 + 11:]
-    else:
-        enc, kvg = rest[:2]
-        scratch = rest[2:]
-    (
-        pas_ref, ask_ref, nb_own, nbg, nbs, picks, got, swap, cop, mem, wq, wo, query, mixed,
-        local_sem, nb_sem, pas_sem, swap_sem, w_sem, enc_sem, ring_sem, twin_sem,
-    ) = scratch
     me = lax.axis_index("span")
     head = lax.axis_index("head")
     group = lax.axis_index("groups")
@@ -149,12 +141,6 @@
     barrier, greeted = greet_all(n)
     pl.semaphore_signal(barrier, inc=1, device_id={"groups": twin}, device_id_type=MESH)
     loads = [pltpu.make_async_copy(pas_in, pas_ref, local_sem.at[7])]
-    if fused:
-        loads += [
-            pltpu.make_async_copy(ask_in, ask_ref, local_sem.at[8]),
-            pltpu.make_async_copy(w_in, tail[0], local_sem.at[9]),
-            pltpu.make_async_copy(states_in, tail[1], local_sem.at[10]),
-        ]
     for copy in loads:
         copy.start()
     nb_own[...] = jnp.zeros_like(nb_own)
@@ -273,39 +259,331 @@
         arrivals.append(ring.advance(2, to_twin))
     enc_copy.wait_recv()
 
-    if fused:
-        loads[1].wait()
-        asks = ask_ref.shape[0]
-        dec_mask = same_span((asks, NB * rows), CT, PT, spans)
-
-        def attend(block):
-            for m in range(kv_ref.shape[2] // HD):
-                flat = enc[...].reshape(NB * rows, width)
-                lanes = pl.ds(m * HD, HD)
-                keys = dot(flat, kvg[block, 0, :, lanes]).astype(jnp.bfloat16)
-                vals = dot(flat, kvg[block, 1, :, lanes]).astype(jnp.bfloat16)
-                spot = pl.ds(pl.multiple_of(block * kv_ref.shape[2] + m * HD, HD), HD)
-                scores = dot(ask_ref[:, spot], keys, ((1,), (1,))) * (1.0 / math.sqrt(HD))
-                att_ref[:, spot] = dot(weigh(scores, dec_mask), vals).astype(jnp.bfloat16)
-
-        attend(me)
-
     for t in range(ring.steps):
         while len(arrivals) < min(t + 3, ring.steps):
             arrivals.append(ring.advance(len(arrivals), to_twin))
         for copy in twins[t]:
             copy.wait_recv()
-        if fused:
-            for block in arrivals[t]:
-                attend(block)
-    if fused:
-        loads[2].wait()
-        loads[3].wait()
-        out_stage(n, att_ref, tail[0], tail[1], out_ref, *tail[2:])
     enc_copy.wait_send()
     for copy in pas_copies + [copy for pair in twins for copy in pair]:
         copy.wait_send()
     ring.finish()
+
+
+def line_order(z, length, j):
+    far_half = z // max(1, length // 2)
+    short = (1 - far_half) * z + far_half * (length - 1 - z)
+    way = 1 - 2 * far_half
+    both = (2 * short - j + 2 * length) // (2 * length)
+    turn = 1 - 2 * (j % 2)
+    source = z + both * turn * way * ((j + 1) // 2) + (1 - both) * way * (j - short)
+    travel = -(both * turn * way + (1 - both) * way)
+    return source, travel
+
+
+def span_kernel(
+    n, spans, nb_ref, pas_in, mem_ref, wq_ref, wo_ref, kv_ref, ask_in, w_in, states_in, out_ref,
+    enc, kvg, att_ref, w_all, states_ref, gathered, partial, crossed, summed, back,
+    pas_ref, ask_ref, nb_own, nbg, nbs, picks, got, swap, cop, mem, wq, wo, query, mixed,
+    local_sem, nb_sem, pas_sem, swap_sem, w_sem, enc_sem, kvz_sem, kvy_sem, kvx_sem,
+    wy_sem, wx_sem, att_sem, fwd_sem, cross_sem, send_sem, back_sem,
+):
+    me = lax.axis_index("span")
+    head = lax.axis_index("head")
+    group = lax.axis_index("groups")
+    other = 1 - head
+    twin = group + 1 - 2 * (group % 2)
+    plane = group % 2
+    length = n // 2
+    z, y = me // 2, me % 2
+    half_rows = PT // 2
+    half_e = wq_ref.shape[0]
+    pending = []
+
+    def go(copy, cond=None):
+        if cond is None:
+            copy.start()
+        else:
+            pl.when(cond)(copy.start)
+        pending.append((copy, cond))
+
+    barrier, greeted = greet_all(n)
+    pl.semaphore_signal(barrier, inc=1, device_id={"groups": twin}, device_id_type=MESH)
+    loads = [
+        pltpu.make_async_copy(pas_in, pas_ref, local_sem.at[7]),
+        pltpu.make_async_copy(ask_in, ask_ref, local_sem.at[8]),
+        pltpu.make_async_copy(w_in, w_all.at[y], local_sem.at[9]),
+        pltpu.make_async_copy(states_in, states_ref, local_sem.at[10]),
+    ]
+    for copy in loads:
+        copy.start()
+    nb_own[...] = jnp.zeros_like(nb_own)
+    nb_own[:spans, :NB] = nb_ref[...]
+    pl.semaphore_wait(barrier, greeted + 1)
+
+    for d in range(1, n):
+        go(remote(nb_own, nbg.at[me], nb_sem.at[0, d], nb_sem.at[1, d], span=(me + d) % n))
+    own_nb = pltpu.make_async_copy(nb_own, nbg.at[me], local_sem.at[0])
+    own_nb.start()
+
+    depth = kv_ref.shape[0]
+    half, extra = depth // 2, depth // 56 * 3
+    plane_lines = pl.ds(pl.multiple_of(plane * (half - extra), 16), half + extra)
+    cross_lines = pl.ds(pl.multiple_of(plane * (half + extra), 16), half - extra)
+
+    def along(source, travel, own):
+        spot = kvg.at[2 * source + y, plane_lines]
+        nxt = z + travel
+        lane = (1 - travel) // 2
+        copy = remote(
+            kv_ref.at[plane_lines] if own else spot, spot, kvz_sem.at[0, source, lane], kvz_sem.at[1, source, lane],
+            span=2 * ((nxt + length) % length) + y,
+        )
+        go(copy, (nxt >= 0) & (nxt < length))
+
+    def to_pair(source, own):
+        spot = kvg.at[2 * source + y, plane_lines]
+        go(remote(
+            kv_ref.at[plane_lines] if own else spot, spot, kvy_sem.at[0, source], kvy_sem.at[1, source],
+            span=2 * z + 1 - y,
+        ))
+
+    def to_twin(block):
+        spot = kvg.at[block, cross_lines]
+        go(remote(spot, spot, kvx_sem.at[0, block], kvx_sem.at[1, block], groups=twin))
+
+    def line_arrival(j):
+        source, travel = line_order(z, length, j)
+        lane = (1 - travel) // 2
+        block = 2 * source + y
+        spot = kvg.at[block, plane_lines]
+        remote(spot, spot, kvz_sem.at[0, source, lane], kvz_sem.at[1, source, lane], span=2 * z + 1 - y).wait_recv()
+        along(source, travel, False)
+        to_pair(source, False)
+        to_twin(block)
+
+    def pair_arrival(j):
+        source = z if j == 0 else line_order(z, length, j)[0]
+        block = 2 * source + 1 - y
+        spot = kvg.at[block, plane_lines]
+        remote(spot, spot, kvy_sem.at[0, source], kvy_sem.at[1, source], span=2 * z + 1 - y).wait_recv()
+        to_twin(block)
+
+    def twin_arrival(block):
+        lines = pl.ds(pl.multiple_of((1 - plane) * (half + extra), 16), half - extra)
+        spot = kvg.at[block, lines]
+        remote(spot, spot, kvx_sem.at[0, block], kvx_sem.at[1, block], groups=twin).wait_recv()
+
+    for travel in (1, -1):
+        along(z, travel, True)
+    to_pair(z, True)
+
+    mine = pl.ds(pl.multiple_of(head * half_e, half_e), half_e)
+    w_copies, own_copies = [], []
+    for i, (src, dst) in enumerate((
+        (mem_ref.at[0], mem.at[0, mine]), (mem_ref.at[1], mem.at[1, mine]), (wq_ref, wq.at[mine]), (wo_ref, wo.at[mine]),
+    )):
+        w_copies.append(remote(src, dst, w_sem.at[0, i], w_sem.at[1, i], head=other))
+        w_copies[-1].start()
+        own_copies.append(pltpu.make_async_copy(src, dst, local_sem.at[3 + i]))
+        own_copies[-1].start()
+    own_copies.append(pltpu.make_async_copy(kv_ref, kvg.at[me], local_sem.at[1]))
+    own_copies[-1].start()
+    own_nb.wait()
+    loads[0].wait()
+    for d in range(1, n):
+        pending[d - 1][0].wait_recv()
+    to_scalar = pltpu.make_async_copy(nbg, nbs, local_sem.at[2])
+    to_scalar.start()
+    to_scalar.wait()
+
+    def pick(requester):
+        index = jnp.int32(0)
+        for e in range(spans * NB):
+            wanted = nbs[requester, e // NB, e % NB]
+            index = index + jnp.where(wanted // PS_DEV == me, wanted % PS_DEV, 0)
+        return pas_ref[index, head]
+
+    pas_copies = []
+    picks[1] = pick((me + 1) % n)
+    for d in range(1, n):
+        if d + 1 < n:
+            picks[d + 1] = pick((me + d + 1) % n)
+        else:
+            got[me] = pick(me)
+        copy = remote(picks.at[d], got.at[me], pas_sem.at[0, d], pas_sem.at[1, d], span=(me + d) % n)
+        go(copy)
+        pas_copies.append(copy)
+
+    w_half = w_in.shape[0] // 2
+    w_lines = pl.ds(pl.multiple_of(plane * w_half, 16), w_half)
+    if length > 1:
+        line_arrival(1)
+    pair_arrival(0)
+    w_pair = remote(w_in.at[w_lines], w_all.at[y, w_lines], wy_sem.at[0], wy_sem.at[1], span=2 * z + 1 - y)
+    go(w_pair)
+    for j in range(2, length):
+        line_arrival(j)
+        pair_arrival(j - 1)
+
+    for copy in pas_copies:
+        copy.wait_recv()
+    swaps = []
+    for c in range(spans):
+        swap[c] = got[nbs[me, c, other] // PS_DEV]
+    for c in range(spans):
+        spot = cop.at[pl.ds(pl.multiple_of(c * PT + head * half_rows, half_rows), half_rows)]
+        copy = remote(swap.at[c], spot, swap_sem.at[0, c], swap_sem.at[1, c], head=other)
+        copy.start()
+        swaps.append(copy)
+        spot[...] = got[nbs[me, c, head] // PS_DEV]
+    for copy in own_copies:
+        copy.wait()
+    for copy in w_copies:
+        copy.wait()
+    for copy in swaps:
+        copy.wait()
+
+    rows = cop.shape[0]
+    tokens = mem.shape[2]
+    width = cop.shape[1]
+    values = cop[...].astype(jnp.float32)
+    query[...] = dot(rms_rows(values).astype(jnp.bfloat16), wq[...], ((1,), (1,))).astype(jnp.bfloat16)
+    mask = same_span((rows, tokens), PT, CT, spans)
+    feature = lax.broadcasted_iota(jnp.int32, (2 * EHD, tokens), 0) // EHD
+    for j in range(width // (2 * EHD)):
+        lines = pl.ds(j * 2 * EHD, 2 * EHD)
+        total = None
+        for e in range(2):
+            keys = jnp.where(feature == e, mem[0, lines], jnp.bfloat16(0))
+            vals = jnp.where(feature == e, mem[1, lines], jnp.bfloat16(0))
+            scores = dot(query[:, lines], keys) * (1.0 / math.sqrt(EHD))
+            term = dot(weigh(scores, mask), vals, ((1,), (1,)))
+            total = term if e == 0 else total + term
+        mixed[:, lines] = total.astype(jnp.bfloat16)
+    branch = dot(mixed[...], wo[...])
+    enc[head] = rms_rows(cop[...].astype(jnp.float32) + branch).astype(jnp.bfloat16)
+    enc_copy = remote(enc.at[head], enc.at[head], enc_sem.at[0], enc_sem.at[1], head=other)
+    go(enc_copy)
+    if length > 1:
+        pair_arrival(length - 1)
+    enc_copy.wait_recv()
+
+    loads[1].wait()
+    asks = ask_ref.shape[0]
+    dec_mask = same_span((asks, NB * rows), CT, PT, spans)
+
+    def send_attended(block):
+        for travel in (1, -1):
+            nxt = z + travel
+            lane = (1 - travel) // 2
+            copy = remote(
+                att_ref.at[block], gathered.at[z, block], att_sem.at[0, lane, block], att_sem.at[1, lane, z],
+                span=2 * ((nxt + length) % length) + y,
+            )
+            go(copy, (nxt >= 0) & (nxt < length))
+
+    def attend(block):
+        flat = enc[...].reshape(NB * rows, width)
+        both = dot(flat, kvg[block]).astype(jnp.bfloat16)
+        spot = pl.ds(pl.multiple_of(block * HD, HD), HD)
+        scores = dot(ask_ref[:, spot], both[:, :HD], ((1,), (1,))) * (1.0 / math.sqrt(HD))
+        att_ref[block] = dot(weigh(scores, dec_mask), both[:, HD:]).astype(jnp.bfloat16)
+        send_attended(block)
+
+    attend(me)
+    w_back = pl.ds(pl.multiple_of((1 - plane) * w_half, 16), w_half)
+    w_pair.wait_recv()
+    crossing_w = w_all.at[1 - y, w_lines]
+    go(remote(crossing_w, crossing_w, wx_sem.at[0], wx_sem.at[1], groups=twin))
+    for j in range(length):
+        if j:
+            block = 2 * line_order(z, length, j)[0] + y
+            twin_arrival(block)
+            attend(block)
+        block = 2 * (line_order(z, length, j)[0] if j else z) + 1 - y
+        twin_arrival(block)
+        attend(block)
+
+    owner_head = z // (length // 2)
+    column = z % (length // 2)
+    out_rows = asks // 2
+    w_width = w_in.shape[1]
+    crossings, returns = [], []
+    loads[2].wait()
+    loads[3].wait()
+    remote(
+        w_all.at[1 - y, w_back], w_all.at[1 - y, w_back], wx_sem.at[0], wx_sem.at[1], groups=twin,
+    ).wait_recv()
+
+    def project(place, rows_ref):
+        i = len(crossings)
+        whole = jnp.concatenate([rows_ref[m] for m in range(n)], axis=1)
+        for k in range(2):
+            value = dot(whole, w_all[k]).astype(jnp.bfloat16)
+            lanes = pl.ds(k * w_width, w_width)
+            partial[i, 0, :, lanes] = value[:out_rows]
+            partial[i, 1, :, lanes] = value[out_rows:]
+        copy = remote(partial.at[i, other], crossed.at[i], cross_sem.at[0, i], cross_sem.at[1, i], head=other)
+        go(copy)
+        crossings.append((copy, place))
+
+    def give_back():
+        i = len(returns)
+        copy, place = crossings[i]
+        copy.wait_recv()
+        total = partial[i, head].astype(jnp.float32) + crossed[i].astype(jnp.float32)
+        summed[i] = total.astype(jnp.bfloat16)
+        copy = remote(
+            summed.at[i], back.at[column, head], send_sem.at[i], back_sem.at[column, head],
+            span=2 * place + y, head=owner_head,
+        )
+        if i == 0:
+            @pl.when(head == owner_head)
+            def _():
+                back[column, head] = summed[i]
+
+            go(copy, head != owner_head)
+        else:
+            go(copy)
+        returns.append(copy)
+
+    project(z, att_ref)
+    for j in range(1, length):
+        source, travel = line_order(z, length, j)
+        lane = (1 - travel) // 2
+        slot = gathered.at[source]
+        nxt = z + travel
+        remote(slot, slot, att_sem.at[0, lane, 0], att_sem.at[1, lane, source], span=2 * z + 1 - y).wait_recv()
+        copy = remote(
+            slot, slot, fwd_sem.at[j], att_sem.at[1, lane, source], span=2 * ((nxt + length) % length) + y,
+        )
+        go(copy, (nxt >= 0) & (nxt < length))
+        project(source, slot)
+        give_back()
+    give_back()
+
+    wide = 2 * w_width
+    for j in range(length // 2):
+        for source in range(2):
+            local = (head * (length // 2) + j == z) & (head == source)
+
+            @pl.when(jnp.logical_not(local))
+            def _():
+                remote(
+                    summed.at[0], back.at[j, source], send_sem.at[0], back_sem.at[j, source], head=other,
+                ).wait_recv()
+
+            lanes = pl.ds(j * wide, wide)
+            lines = pl.ds(source * out_rows, out_rows)
+            out_ref[lines, lanes] = (
+                states_ref[lines, lanes].astype(jnp.float32) + back[j, source].astype(jnp.float32)
+            ).astype(jnp.bfloat16)
+    for copy, cond in pending:
+        if cond is None:
+            copy.wait_send()
+        else:
+            pl.when(cond)(copy.wait_send)
 
 
 def out_kernel(n, *refs):
@@ -451,27 +729,14 @@
     bf16 = jnp.bfloat16
     dma = pltpu.SemaphoreType.DMA
     half_rows = PT // 2
-    kv = kv_weight.transpose(1, 0, 2)
     memory = span_memory.transpose(1, 2, 0)
     rows, tokens = span_count * PT, span_memory.shape[0]
     sds = jax.ShapeDtypeStruct
-    fused = kv.shape[2] % HD == 0
-    enc_shape, kv_shape = (NB, rows, E), (n,) + kv.shape
     states, width = sds(span_states.shape, bf16), out_weight.shape[1]
-    out_scratch = [
-        pltpu.VMEM((n,) + span_queries.shape, bf16),
-        pltpu.VMEM((n, 2, tokens // 2, width), bf16),
-        pltpu.VMEM((n, tokens // 2, width), bf16),
-        pltpu.VMEM((n, tokens // 2, width), bf16),
-        pltpu.VMEM((n // 2, 2, tokens // 2, width), bf16),
-        dma((2, 2, n // 2, 2)),
-        dma((2, n)),
-        dma((n,)),
-        dma((n // 2, 2)),
-    ]
+    half = tokens // 2
+    operands = (neighbours, passages.reshape(-1, 2, half_rows, E), memory, enc_query_w.T, enc_out_w.T)
+    pas_scratch = [pltpu.VMEM((passages.shape[0] // PT, 2, half_rows, E), bf16)]
     scratch = [
-        pltpu.VMEM((passages.shape[0] // PT, 2, half_rows, E), bf16),
-        pltpu.VMEM(span_queries.shape if fused else (16, 128), bf16),
         pltpu.VMEM((8, 128), jnp.int32),
         pltpu.VMEM((n, 8, 128), jnp.int32),
         pltpu.SMEM((n, 8, 128), jnp.int32),
@@ -490,23 +755,57 @@
         dma((2, span_count)),
         dma((2, 4)),
         dma((2,)),
-        dma((2, 2, n // 2, 4)),
+    ]
+    if kv_weight.shape[2] == HD and n % 4 == 0:
+        length = n // 2
+        line_scratch = [
+            pltpu.VMEM((NB, rows, E), bf16),
+            pltpu.VMEM((n, E, 2 * HD), bf16),
+            pltpu.VMEM((n, tokens, HD), bf16),
+            pltpu.VMEM((2,) + out_weight.shape, bf16),
+            pltpu.VMEM(span_states.shape, bf16),
+            pltpu.VMEM((length, n, tokens, HD), bf16),
+            pltpu.VMEM((length, 2, half, 2 * width), bf16),
+            pltpu.VMEM((length, half, 2 * width), bf16),
+            pltpu.VMEM((length, half, 2 * width), bf16),
+            pltpu.VMEM((length // 2, 2, half, 2 * width), bf16),
+        ]
+        line_sems = [
+            dma((2, length, 2)),
+            dma((2, length)),
+            dma((2, n)),
+            dma((2,)),
+            dma((2,)),
+            dma((2, 2, n)),
+            dma((length,)),
+            dma((2, length)),
+            dma((length,)),
+            dma((length // 2, 2)),
+        ]
+        return call(
+            functools.partial(span_kernel, n, span_count), 2, [states],
+            line_scratch + pas_scratch + [pltpu.VMEM(span_queries.shape, bf16)] + scratch + line_sems,
+            [pltpu.VMEM] + [pl.ANY] * 8,
+            *operands, kv_weight.reshape(E, 2 * HD), span_queries, out_weight, span_states,
+        )[0]
+    kv = kv_weight.transpose(1, 0, 2)
+    out_scratch = [
+        pltpu.VMEM((n,) + span_queries.shape, bf16),
+        pltpu.VMEM((n, 2, half, width), bf16),
+        pltpu.VMEM((n, half, width), bf16),
+        pltpu.VMEM((n, half, width), bf16),
+        pltpu.VMEM((n // 2, 2, half, width), bf16),
         dma((2, 2, n // 2, 2)),
+        dma((2, n)),
+        dma((n,)),
+        dma((n // 2, 2)),
     ]
-    if fused:
-        scratch = [
-            pltpu.VMEM(enc_shape, bf16), pltpu.VMEM(kv_shape, bf16), pltpu.VMEM(span_queries.shape, bf16),
-            pltpu.VMEM(out_weight.shape, bf16), pltpu.VMEM(span_states.shape, bf16),
-        ] + out_scratch + scratch
     found = call(
-        functools.partial(fetch_kernel, n, lax.axis_size("groups"), span_count, fused), 0,
-        [states] if fused else [sds(enc_shape, bf16), sds(kv_shape, bf16)],
-        scratch, [pltpu.VMEM] + [pl.ANY] * 8,
-        neighbours, passages.reshape(-1, 2, half_rows, E), memory, enc_query_w.T, enc_out_w.T, kv,
-        span_queries, out_weight, span_states,
+        functools.partial(fetch_kernel, n, span_count), 0,
+        [sds((NB, rows, E), bf16), sds((n,) + kv.shape, bf16)],
+        pas_scratch + scratch + [dma((2, 2, n // 2, 4)), dma((2, 2, n // 2, 2))], [pltpu.VMEM] + [pl.ANY] * 5,
+        *operands, kv,
     )
-    if fused:
-        return found[0]
     attended = decode(found[0], found[1], span_queries, span_count)
     return call(
         functools.partial(out_kernel, n), 1, [states], out_scratch, [pltpu.VMEM] * 3,

time: 102 us -> 103 us (level)
  no operation moved by 1% of the time
where the time goes in v1:
time: 103 us
  Pallas kernels  99 us (96%)
  local copies, waits for them, and re-layouts  3.74 us (4%)
    pallas_call x1, Pallas kernels, call(): pl.pallas_call(kernel, out_shape=out_shape, in_specs=[pl.BlockSpec(memory...  99 us
    unnamed x2, local copies, waits for them, and re-layouts  3.74 us

profile of v1, /device:TPU:1, one launch (start us, length us, event | category | flops | bytes accessed | tf_op | source)
XLA Modules:
  0.0 102.7 jit_solution(14149658895946349041)
XLA Ops:
  0.0 1.9 %copy.12 = bf16[112,8,2,128]{3,1,2,0:T(8,128)(2,1)} copy(bf16[112,8,2,128]{3,2,1,0:T(2,128)(2,1)} %bitcast.12) | data formatting | bytes 917504
  1.9 99.0 %shard_map.91 = bf16[128,2048]{1,0:T(8,128)(2,1)} custom-call(s32[2,2]{1,0:T(2,128)} %nb_ref.1, bf16[8,2,64,896]{3,2,1,0:T(8,128)(2,1)} %bitcast.9, bf16[2,448,128]{2,1,0:T(8,128)(2,1)} %bitcast.13, bf16[448,896]{1,0:T(8,128)(2,1)} %bitcast.10, bf16[448,896]{1,0:T(8,128)(2,1)} %bitcast.11, bf16[896,256]{1,0:T(8,128)(2,1)} %bitcast.8, ...), custom_call_target="tpu_custom_call" | custom-call | tf_op jit(solution)/shard_map/pallas_call | solution.py:687
  100.8 1.9 %copy.14 = bf16[128,2048]{1,0:T(8,128)(2,1)} copy(bf16[128,2048]{1,0:T(8,128)(2,1)} %shard_map.91) | data formatting | bytes 1048576

commit v2 on v1

--- a/solution.py
+++ b/solution.py
@@ -270,6 +270,12 @@
     ring.finish()
 
 
+W_CUTS = 4
+W_CROSS = 1
+KV_EXTRA = 6
+KV_CUTS = 2
+
+
 def line_order(z, length, j):
     far_half = z // max(1, length // 2)
     short = (1 - far_half) * z + far_half * (length - 1 - z)
@@ -286,7 +292,7 @@
     enc, kvg, att_ref, w_all, states_ref, gathered, partial, crossed, summed, back,
     pas_ref, ask_ref, nb_own, nbg, nbs, picks, got, swap, cop, mem, wq, wo, query, mixed,
     local_sem, nb_sem, pas_sem, swap_sem, w_sem, enc_sem, kvz_sem, kvy_sem, kvx_sem,
-    wy_sem, wx_sem, att_sem, fwd_sem, cross_sem, send_sem, back_sem,
+    wy_sem, wx_sem, att_sem, cross_sem, send_sem, back_sem,
 ):
     me = lax.axis_index("span")
     head = lax.axis_index("head")
@@ -300,12 +306,14 @@
     half_e = wq_ref.shape[0]
     pending = []
 
-    def go(copy, cond=None):
-        if cond is None:
-            copy.start()
-        else:
-            pl.when(cond)(copy.start)
-        pending.append((copy, cond))
+    def go(copy, cond=None, start=True, note=True):
+        if start:
+            if cond is None:
+                copy.start()
+            else:
+                pl.when(cond)(copy.start)
+        if note:
+            pending.append((copy, cond))
 
     barrier, greeted = greet_all(n)
     pl.semaphore_signal(barrier, inc=1, device_id={"groups": twin}, device_id_type=MESH)
@@ -327,56 +335,77 @@
     own_nb.start()
 
     depth = kv_ref.shape[0]
-    half, extra = depth // 2, depth // 56 * 3
-    plane_lines = pl.ds(pl.multiple_of(plane * (half - extra), 16), half + extra)
-    cross_lines = pl.ds(pl.multiple_of(plane * (half + extra), 16), half - extra)
-
-    def along(source, travel, own):
-        spot = kvg.at[2 * source + y, plane_lines]
+    half, extra = depth // 2, depth // 56 * KV_EXTRA
+    cut = (half + extra) // KV_CUTS
+    parts = range(KV_CUTS)
+
+    def from_edge(side, offset, size):
+        return pl.ds(pl.multiple_of((1 - side) * offset + side * (depth - offset - size), 16), size)
+
+    def plane_part(i):
+        return from_edge(plane, i * cut, cut)
+
+    def cross_part(side, i):
+        start = min(i * cut, half - extra)
+        return from_edge(side, start, min((i + 1) * cut, half - extra) - start)
+
+    crossed_parts = [i for i in parts if i * cut < half - extra]
+
+    def along(source, travel, i, own, **how):
+        lines = plane_part(i)
+        spot = kvg.at[2 * source + y, lines]
         nxt = z + travel
         lane = (1 - travel) // 2
         copy = remote(
-            kv_ref.at[plane_lines] if own else spot, spot, kvz_sem.at[0, source, lane], kvz_sem.at[1, source, lane],
+            kv_ref.at[lines] if own else spot, spot, kvz_sem.at[0, source, lane, i], kvz_sem.at[1, source, lane, i],
             span=2 * ((nxt + length) % length) + y,
         )
-        go(copy, (nxt >= 0) & (nxt < length))
-
-    def to_pair(source, own):
-        spot = kvg.at[2 * source + y, plane_lines]
+        go(copy, (nxt >= 0) & (nxt < length), **how)
+
+    def to_pair(source, i, own, **how):
+        lines = plane_part(i)
+        spot = kvg.at[2 * source + y, lines]
         go(remote(
-            kv_ref.at[plane_lines] if own else spot, spot, kvy_sem.at[0, source], kvy_sem.at[1, source],
+            kv_ref.at[lines] if own else spot, spot, kvy_sem.at[0, source, i], kvy_sem.at[1, source, i],
             span=2 * z + 1 - y,
-        ))
-
-    def to_twin(block):
-        spot = kvg.at[block, cross_lines]
-        go(remote(spot, spot, kvx_sem.at[0, block], kvx_sem.at[1, block], groups=twin))
-
-    def line_arrival(j):
+        ), **how)
+
+    def to_twin(block, i, **how):
+        if i in crossed_parts:
+            spot = kvg.at[block, cross_part(plane, i)]
+            go(remote(spot, spot, kvx_sem.at[0, block, i], kvx_sem.at[1, block, i], groups=twin), **how)
+
+    def line_arrival(j, start=True, note=True):
         source, travel = line_order(z, length, j)
         lane = (1 - travel) // 2
         block = 2 * source + y
-        spot = kvg.at[block, plane_lines]
-        remote(spot, spot, kvz_sem.at[0, source, lane], kvz_sem.at[1, source, lane], span=2 * z + 1 - y).wait_recv()
-        along(source, travel, False)
-        to_pair(source, False)
-        to_twin(block)
+        for i in parts:
+            spot = kvg.at[block, plane_part(i)]
+            if start:
+                remote(
+                    spot, spot, kvz_sem.at[0, source, lane, i], kvz_sem.at[1, source, lane, i], span=2 * z + 1 - y,
+                ).wait_recv()
+            along(source, travel, i, False, start=start, note=note)
+            to_pair(source, i, False, start=start, note=note)
+            to_twin(block, i, start=start, note=note)
 
     def pair_arrival(j):
         source = z if j == 0 else line_order(z, length, j)[0]
         block = 2 * source + 1 - y
-        spot = kvg.at[block, plane_lines]
-        remote(spot, spot, kvy_sem.at[0, source], kvy_sem.at[1, source], span=2 * z + 1 - y).wait_recv()
-        to_twin(block)
+        for i in parts:
+            spot = kvg.at[block, plane_part(i)]
+            remote(spot, spot, kvy_sem.at[0, source, i], kvy_sem.at[1, source, i], span=2 * z + 1 - y).wait_recv()
+            to_twin(block, i)
 
     def twin_arrival(block):
-        lines = pl.ds(pl.multiple_of((1 - plane) * (half + extra), 16), half - extra)
-        spot = kvg.at[block, lines]
-        remote(spot, spot, kvx_sem.at[0, block], kvx_sem.at[1, block], groups=twin).wait_recv()
-
-    for travel in (1, -1):
-        along(z, travel, True)
-    to_pair(z, True)
+        for i in crossed_parts:
+            spot = kvg.at[block, cross_part(1 - plane, i)]
+            remote(spot, spot, kvx_sem.at[0, block, i], kvx_sem.at[1, block, i], groups=twin).wait_recv()
+
+    for i in parts:
+        for travel in (1, -1):
+            along(z, travel, i, True)
+        to_pair(z, i, True)
 
     mine = pl.ds(pl.multiple_of(head * half_e, half_e), half_e)
     w_copies, own_copies = [], []
@@ -414,18 +443,10 @@
         copy = remote(picks.at[d], got.at[me], pas_sem.at[0, d], pas_sem.at[1, d], span=(me + d) % n)
         go(copy)
         pas_copies.append(copy)
-
-    w_half = w_in.shape[0] // 2
-    w_lines = pl.ds(pl.multiple_of(plane * w_half, 16), w_half)
-    if length > 1:
-        line_arrival(1)
+    line_arrival(1)
     pair_arrival(0)
-    w_pair = remote(w_in.at[w_lines], w_all.at[y, w_lines], wy_sem.at[0], wy_sem.at[1], span=2 * z + 1 - y)
-    go(w_pair)
-    for j in range(2, length):
-        line_arrival(j)
-        pair_arrival(j - 1)
-
+    inner = (z > 0) & (z < length - 1)
+    pl.when(inner)(lambda: line_arrival(2, note=False))
     for copy in pas_copies:
         copy.wait_recv()
     swaps = []
@@ -437,13 +458,15 @@
         copy.start()
         swaps.append(copy)
         spot[...] = got[nbs[me, c, head] // PS_DEV]
+    pl.when(jnp.logical_not(inner))(lambda: line_arrival(2, note=False))
+    line_arrival(2, start=False)
+    pair_arrival(1)
     for copy in own_copies:
         copy.wait()
     for copy in w_copies:
         copy.wait()
     for copy in swaps:
         copy.wait()
-
     rows = cop.shape[0]
     tokens = mem.shape[2]
     width = cop.shape[1]
@@ -465,120 +488,164 @@
     enc[head] = rms_rows(cop[...].astype(jnp.float32) + branch).astype(jnp.bfloat16)
     enc_copy = remote(enc.at[head], enc.at[head], enc_sem.at[0], enc_sem.at[1], head=other)
     go(enc_copy)
-    if length > 1:
-        pair_arrival(length - 1)
+    for j in range(3, length):
+        line_arrival(j)
+        pair_arrival(j - 1)
+    w_chunk = w_in.shape[0] // W_CUTS
+
+    def w_part(side, i):
+        lines = (1 - side) * i + side * (W_CUTS - 1 - i)
+        return pl.ds(pl.multiple_of(lines * w_chunk, 16), w_chunk)
+
+    w_pairs = []
+    for i in range(W_CUTS - W_CROSS):
+        lines = w_part(plane, i)
+        w_pairs.append(remote(
+            w_in.at[lines], w_all.at[y, lines], wy_sem.at[0, i], wy_sem.at[1, i], span=2 * z + 1 - y,
+        ))
+        go(w_pairs[-1])
+
+    def w_forward(i):
+        w_pairs[i].wait_recv()
+        spot = w_all.at[1 - y, w_part(plane, i)]
+        go(remote(spot, spot, wx_sem.at[0, i], wx_sem.at[1, i], groups=twin))
+
+    def w_arrival(i):
+        spot = w_all.at[1 - y, w_part(1 - plane, i)]
+        remote(spot, spot, wx_sem.at[0, i], wx_sem.at[1, i], groups=twin).wait_recv()
     enc_copy.wait_recv()
 
     loads[1].wait()
     asks = ask_ref.shape[0]
-    dec_mask = same_span((asks, NB * rows), CT, PT, spans)
-
-    def send_attended(block):
+    def send_attended(place):
+        spot = pl.ds(2 * place, 2)
         for travel in (1, -1):
             nxt = z + travel
             lane = (1 - travel) // 2
             copy = remote(
-                att_ref.at[block], gathered.at[z, block], att_sem.at[0, lane, block], att_sem.at[1, lane, z],
+                att_ref.at[spot], gathered.at[z, spot], att_sem.at[0, lane, z, place], att_sem.at[1, lane, z, place],
                 span=2 * ((nxt + length) % length) + y,
             )
             go(copy, (nxt >= 0) & (nxt < length))
 
+    dec_mask = same_span((asks, NB * rows), CT, PT, spans)
+
     def attend(block):
         flat = enc[...].reshape(NB * rows, width)
-        both = dot(flat, kvg[block]).astype(jnp.bfloat16)
+        keys = dot(flat, kvg[block, :, pl.ds(0, HD)]).astype(jnp.bfloat16)
+        vals = dot(flat, kvg[block, :, pl.ds(HD, HD)]).astype(jnp.bfloat16)
         spot = pl.ds(pl.multiple_of(block * HD, HD), HD)
-        scores = dot(ask_ref[:, spot], both[:, :HD], ((1,), (1,))) * (1.0 / math.sqrt(HD))
-        att_ref[block] = dot(weigh(scores, dec_mask), both[:, HD:]).astype(jnp.bfloat16)
-        send_attended(block)
-
-    attend(me)
-    w_back = pl.ds(pl.multiple_of((1 - plane) * w_half, 16), w_half)
-    w_pair.wait_recv()
-    crossing_w = w_all.at[1 - y, w_lines]
-    go(remote(crossing_w, crossing_w, wx_sem.at[0], wx_sem.at[1], groups=twin))
+        scores = dot(ask_ref[:, spot], keys, ((1,), (1,))) * (1.0 / math.sqrt(HD))
+        att_ref[block] = dot(weigh(scores, dec_mask), vals).astype(jnp.bfloat16)
+
     for j in range(length):
-        if j:
-            block = 2 * line_order(z, length, j)[0] + y
+        source = line_order(z, length, j)[0] if j else z
+        blocks = [2 * source + y, 2 * source + 1 - y]
+        for block in blocks[0 if j else 1:]:
             twin_arrival(block)
+        for block in blocks:
             attend(block)
-        block = 2 * (line_order(z, length, j)[0] if j else z) + 1 - y
-        twin_arrival(block)
-        attend(block)
+        send_attended(source)
+        if j == length - 1:
+            for i in range(W_CROSS):
+                w_forward(i)
+        if j == 0:
+            pair_arrival(length - 1)
 
     owner_head = z // (length // 2)
     column = z % (length // 2)
     out_rows = asks // 2
     w_width = w_in.shape[1]
     crossings, returns = [], []
-    loads[2].wait()
-    loads[3].wait()
-    remote(
-        w_all.at[1 - y, w_back], w_all.at[1 - y, w_back], wx_sem.at[0], wx_sem.at[1], groups=twin,
-    ).wait_recv()
-
-    def project(place, rows_ref):
-        i = len(crossings)
+
+    def attended_arrival(j):
+        source, travel = line_order(z, length, j)
+        lane = (1 - travel) // 2
+        nxt = z + travel
+        for i in range(length):
+            place = line_order(source, length, i)[0] if i else source
+            slot = gathered.at[source, pl.ds(2 * place, 2)]
+            copy = remote(
+                slot, slot, att_sem.at[0, lane, source, place], att_sem.at[1, lane, source, place],
+                span=2 * ((nxt + length) % length) + y,
+            )
+            copy.wait_recv()
+            go(copy, (nxt >= 0) & (nxt < length))
+        return source, gathered.at[source]
+
+    def project(slot, k, rows_ref, place):
         whole = jnp.concatenate([rows_ref[m] for m in range(n)], axis=1)
-        for k in range(2):
-            value = dot(whole, w_all[k]).astype(jnp.bfloat16)
-            lanes = pl.ds(k * w_width, w_width)
-            partial[i, 0, :, lanes] = value[:out_rows]
-            partial[i, 1, :, lanes] = value[out_rows:]
-        copy = remote(partial.at[i, other], crossed.at[i], cross_sem.at[0, i], cross_sem.at[1, i], head=other)
+        value = dot(whole, w_all[k]).astype(jnp.bfloat16)
+        partial[slot, k, 0] = value[:out_rows]
+        partial[slot, k, 1] = value[out_rows:]
+        copy = remote(
+            partial.at[slot, k, other], crossed.at[slot, k], cross_sem.at[0, slot, k], cross_sem.at[1, slot, k], head=other,
+        )
         go(copy)
-        crossings.append((copy, place))
+        crossings.append((copy, slot, k, place))
 
     def give_back():
-        i = len(returns)
-        copy, place = crossings[i]
+        copy, slot, k, place = crossings[len(returns)]
         copy.wait_recv()
-        total = partial[i, head].astype(jnp.float32) + crossed[i].astype(jnp.float32)
-        summed[i] = total.astype(jnp.bfloat16)
+        total = partial[slot, k, head].astype(jnp.float32) + crossed[slot, k].astype(jnp.float32)
+        summed[slot, k] = total.astype(jnp.bfloat16)
         copy = remote(
-            summed.at[i], back.at[column, head], send_sem.at[i], back_sem.at[column, head],
+            summed.at[slot, k], back.at[column, head, k], send_sem.at[slot, k], back_sem.at[column, head, k],
             span=2 * place + y, head=owner_head,
         )
-        if i == 0:
+        if slot == 0:
             @pl.when(head == owner_head)
             def _():
-                back[column, head] = summed[i]
+                back[column, head, k] = summed[slot, k]
 
             go(copy, head != owner_head)
         else:
             go(copy)
         returns.append(copy)
 
-    project(z, att_ref)
-    for j in range(1, length):
-        source, travel = line_order(z, length, j)
-        lane = (1 - travel) // 2
-        slot = gathered.at[source]
-        nxt = z + travel
-        remote(slot, slot, att_sem.at[0, lane, 0], att_sem.at[1, lane, source], span=2 * z + 1 - y).wait_recv()
-        copy = remote(
-            slot, slot, fwd_sem.at[j], att_sem.at[1, lane, source], span=2 * ((nxt + length) % length) + y,
-        )
-        go(copy, (nxt >= 0) & (nxt < length))
-        project(source, slot)
-        give_back()
+    loads[2].wait()
+    loads[3].wait()
+    arrived = [(att_ref, z)]
+
+    def arrive(j):
+        source, slot = attended_arrival(j)
+        arrived.append((slot, source))
+
+    def work(slot, k):
+        project(slot, k, *arrived[slot])
+        if len(crossings) > 1:
+            give_back()
+    work(0, y)
+    for j in range(1, length - 1):
+        arrive(j)
+        work(j, y)
+    for i in range(W_CROSS, W_CUTS - W_CROSS):
+        w_pairs[i].wait_recv()
+    for i in range(W_CROSS):
+        w_arrival(i)
+    for j in range(length - 1):
+        work(j, 1 - y)
+    arrive(length - 1)
+    work(length - 1, y)
+    work(length - 1, 1 - y)
     give_back()
 
-    wide = 2 * w_width
     for j in range(length // 2):
         for source in range(2):
-            local = (head * (length // 2) + j == z) & (head == source)
-
-            @pl.when(jnp.logical_not(local))
-            def _():
-                remote(
-                    summed.at[0], back.at[j, source], send_sem.at[0], back_sem.at[j, source], head=other,
-                ).wait_recv()
-
-            lanes = pl.ds(j * wide, wide)
-            lines = pl.ds(source * out_rows, out_rows)
-            out_ref[lines, lanes] = (
-                states_ref[lines, lanes].astype(jnp.float32) + back[j, source].astype(jnp.float32)
-            ).astype(jnp.bfloat16)
+            for k in range(2):
+                local = (head * (length // 2) + j == z) & (head == source)
+
+                @pl.when(jnp.logical_not(local))
+                def _():
+                    remote(
+                        summed.at[0, 0], back.at[j, source, k], send_sem.at[0, 0], back_sem.at[j, source, k], head=other,
+                    ).wait_recv()
+
+                lanes = pl.ds((2 * j + k) * w_width, w_width)
+                lines = pl.ds(source * out_rows, out_rows)
+                out_ref[lines, lanes] = (
+                    states_ref[lines, lanes].astype(jnp.float32) + back[j, source, k].astype(jnp.float32)
+                ).astype(jnp.bfloat16)
     for copy, cond in pending:
         if cond is None:
             copy.wait_send()
@@ -765,22 +832,21 @@
             pltpu.VMEM((2,) + out_weight.shape, bf16),
             pltpu.VMEM(span_states.shape, bf16),
             pltpu.VMEM((length, n, tokens, HD), bf16),
-            pltpu.VMEM((length, 2, half, 2 * width), bf16),
-            pltpu.VMEM((length, half, 2 * width), bf16),
-            pltpu.VMEM((length, half, 2 * width), bf16),
-            pltpu.VMEM((length // 2, 2, half, 2 * width), bf16),
+            pltpu.VMEM((length, 2, 2, half, width), bf16),
+            pltpu.VMEM((length, 2, half, width), bf16),
+            pltpu.VMEM((length, 2, half, width), bf16),
+            pltpu.VMEM((length // 2, 2, 2, half, width), bf16),
         ]
         line_sems = [
+            dma((2, length, 2, KV_CUTS)),
+            dma((2, length, KV_CUTS)),
+            dma((2, n, KV_CUTS)),
+            dma((2, W_CUTS)),
+            dma((2, W_CUTS)),
+            dma((2, 2, length, length)),
             dma((2, length, 2)),
-            dma((2, length)),
-            dma((2, n)),
-            dma((2,)),
-            dma((2,)),
-            dma((2, 2, n)),
-            dma((length,)),
-            dma((2, length)),
-            dma((length,)),
-            dma((length // 2, 2)),
+            dma((length, 2)),
+            dma((length // 2, 2, 2)),
         ]
         return call(
             functools.partial(span_kernel, n, span_count), 2, [states],

time: 103 us -> 92.2 us (0.90)
  Pallas kernels: 99 us -> 87.4 us
    pallas_call x1, Pallas kernels: 99 us -> 87.4 us  [call(): pl.pallas_call(kernel, out_shape=out_shape, in_specs=[pl.BlockSpec(memory...]
where the time goes in v2:
time: 92.2 us; the launch traced here: 91.1 us
  Pallas kernels  87.4 us (95%)
  local copies, waits for them, and re-layouts  3.74 us (4%)
    pallas_call x1, Pallas kernels, call(): pl.pallas_call(kernel, out_shape=out_shape, in_specs=[pl.BlockSpec(memory...  87.4 us
    unnamed x2, local copies, waits for them, and re-layouts  3.74 us

profile of v2, /device:TPU:1, one launch (start us, length us, event | category | flops | bytes accessed | tf_op | source)
XLA Modules:
  0.0 91.1 jit_solution(14016584711492358004)
XLA Ops:
  0.0 1.9 %copy.12 = bf16[112,8,2,128]{3,1,2,0:T(8,128)(2,1)} copy(bf16[112,8,2,128]{3,2,1,0:T(2,128)(2,1)} %bitcast.12) | data formatting | bytes 917504
  1.9 87.4 %shard_map.91 = bf16[128,2048]{1,0:T(8,128)(2,1)} custom-call(s32[2,2]{1,0:T(2,128)} %nb_ref.1, bf16[8,2,64,896]{3,2,1,0:T(8,128)(2,1)} %bitcast.9, bf16[2,448,128]{2,1,0:T(8,128)(2,1)} %bitcast.13, bf16[448,896]{1,0:T(8,128)(2,1)} %bitcast.10, bf16[448,896]{1,0:T(8,128)(2,1)} %bitcast.11, bf16[896,256]{1,0:T(8,128)(2,1)} %bitcast.8, ...), custom_call_target="tpu_custom_call" | custom-call | tf_op jit(solution)/shard_map/pallas_call | solution.py:754
  89.2 1.9 %copy.14 = bf16[128,2048]{1,0:T(8,128)(2,1)} copy(bf16[128,2048]{1,0:T(8,128)(2,1)} %shard_map.91) | data formatting | bytes 1048576

commit v3 on v2

--- a/solution.py
+++ b/solution.py
@@ -276,12 +276,12 @@
 KV_CUTS = 2
 
 
-def line_order(z, length, j):
+def line_order(z, length, j, first=-1):
     far_half = z // max(1, length // 2)
     short = (1 - far_half) * z + far_half * (length - 1 - z)
     way = 1 - 2 * far_half
     both = (2 * short - j + 2 * length) // (2 * length)
-    turn = 1 - 2 * (j % 2)
+    turn = first * (2 * (j % 2) - 1)
     source = z + both * turn * way * ((j + 1) // 2) + (1 - both) * way * (j - short)
     travel = -(both * turn * way + (1 - both) * way)
     return source, travel
@@ -488,9 +488,6 @@
     enc[head] = rms_rows(cop[...].astype(jnp.float32) + branch).astype(jnp.bfloat16)
     enc_copy = remote(enc.at[head], enc.at[head], enc_sem.at[0], enc_sem.at[1], head=other)
     go(enc_copy)
-    for j in range(3, length):
-        line_arrival(j)
-        pair_arrival(j - 1)
     w_chunk = w_in.shape[0] // W_CUTS
 
     def w_part(side, i):
@@ -503,7 +500,6 @@
         w_pairs.append(remote(
             w_in.at[lines], w_all.at[y, lines], wy_sem.at[0, i], wy_sem.at[1, i], span=2 * z + 1 - y,
         ))
-        go(w_pairs[-1])
 
     def w_forward(i):
         w_pairs[i].wait_recv()
@@ -513,6 +509,11 @@
     def w_arrival(i):
         spot = w_all.at[1 - y, w_part(1 - plane, i)]
         remote(spot, spot, wx_sem.at[0, i], wx_sem.at[1, i], groups=twin).wait_recv()
+
+    def far_lines():
+        for k in range(3, length):
+            line_arrival(k, note=False)
+    pl.when(inner)(far_lines)
     enc_copy.wait_recv()
 
     loads[1].wait()
@@ -550,6 +551,13 @@
             for i in range(W_CROSS):
                 w_forward(i)
         if j == 0:
+            pl.when(jnp.logical_not(inner))(far_lines)
+            for k in range(3, length):
+                line_arrival(k, start=False)
+                pair_arrival(k - 1)
+            for copy in w_pairs:
+                go(copy)
+        if j == 1:
             pair_arrival(length - 1)
 
     owner_head = z // (length // 2)
@@ -558,8 +566,8 @@
     w_width = w_in.shape[1]
     crossings, returns = [], []
 
-    def attended_arrival(j):
-        source, travel = line_order(z, length, j)
+    def attended_arrival(j, start=True, note=True):
+        source, travel = line_order(z, length, j, 1)
         lane = (1 - travel) // 2
         nxt = z + travel
         for i in range(length):
@@ -569,9 +577,9 @@
                 slot, slot, att_sem.at[0, lane, source, place], att_sem.at[1, lane, source, place],
                 span=2 * ((nxt + length) % length) + y,
             )
-            copy.wait_recv()
-            go(copy, (nxt >= 0) & (nxt < length))
-        return source, gathered.at[source]
+            if start:
+                copy.wait_recv()
+            go(copy, (nxt >= 0) & (nxt < length), start=start, note=note)
 
     def project(slot, k, rows_ref, place):
         whole = jnp.concatenate([rows_ref[m] for m in range(n)], axis=1)
@@ -607,9 +615,12 @@
     loads[3].wait()
     arrived = [(att_ref, z)]
 
-    def arrive(j):
-        source, slot = attended_arrival(j)
-        arrived.append((slot, source))
+    for j in range(1, length):
+        source = line_order(z, length, j, 1)[0]
+        arrived.append((gathered.at[source], source))
+
+    def last_arrival():
+        attended_arrival(length - 1, note=False)
 
     def work(slot, k):
         project(slot, k, *arrived[slot])
@@ -617,19 +628,22 @@
             give_back()
     work(0, y)
     for j in range(1, length - 1):
-        arrive(j)
+        attended_arrival(j)
         work(j, y)
+    pl.when(inner)(last_arrival)
     for i in range(W_CROSS, W_CUTS - W_CROSS):
         w_pairs[i].wait_recv()
     for i in range(W_CROSS):
         w_arrival(i)
     for j in range(length - 1):
         work(j, 1 - y)
-    arrive(length - 1)
+    pl.when(jnp.logical_not(inner))(last_arrival)
+    attended_arrival(length - 1, start=False)
     work(length - 1, y)
     work(length - 1, 1 - y)
     give_back()
 
+    stored = []
     for j in range(length // 2):
         for source in range(2):
             for k in range(2):
@@ -643,9 +657,16 @@
 
                 lanes = pl.ds((2 * j + k) * w_width, w_width)
                 lines = pl.ds(source * out_rows, out_rows)
-                out_ref[lines, lanes] = (
+                states_ref[lines, lanes] = (
                     states_ref[lines, lanes].astype(jnp.float32) + back[j, source, k].astype(jnp.float32)
                 ).astype(jnp.bfloat16)
+                copy = pltpu.make_async_copy(
+                    states_ref.at[lines, lanes], out_ref.at[lines, lanes], local_sem.at[11 + len(stored)],
+                )
+                copy.start()
+                stored.append(copy)
+    for copy in stored:
+        copy.wait()
     for copy, cond in pending:
         if cond is None:
             copy.wait_send()
@@ -750,12 +771,12 @@
             copy.wait_send()
 
 
-def call(kernel, collective_id, out_shape, scratch_shapes, spaces, *operands):
+def call(kernel, collective_id, out_shape, scratch_shapes, spaces, *operands, out_space=pltpu.VMEM):
     return pl.pallas_call(
         kernel,
         out_shape=out_shape,
         in_specs=[pl.BlockSpec(memory_space=space) for space in spaces],
-        out_specs=[pl.BlockSpec(memory_space=pltpu.VMEM)] * len(out_shape),
+        out_specs=[pl.BlockSpec(memory_space=out_space)] * len(out_shape),
         scratch_shapes=scratch_shapes,
         compiler_params=pltpu.CompilerParams(collective_id=collective_id, has_side_effects=True),
     )(*operands)
@@ -816,7 +837,7 @@
         pltpu.VMEM((E, E), bf16),
         pltpu.VMEM((rows, E), bf16),
         pltpu.VMEM((rows, E), bf16),
-        dma((11,)),
+        dma((11 + 4 * n,)),
         dma((2, n)),
         dma((2, n)),
         dma((2, span_count)),
@@ -853,6 +874,7 @@
             line_scratch + pas_scratch + [pltpu.VMEM(span_queries.shape, bf16)] + scratch + line_sems,
             [pltpu.VMEM] + [pl.ANY] * 8,
             *operands, kv_weight.reshape(E, 2 * HD), span_queries, out_weight, span_states,
+            out_space=pl.ANY,
         )[0]
     kv = kv_weight.transpose(1, 0, 2)
     out_scratch = [

time: 92.2 us -> 85.4 us (0.926)
  Pallas kernels: 87.4 us -> 81.4 us
    pallas_call x1, Pallas kernels: 87.4 us -> 81.4 us  [call(): pl.pallas_call(kernel, out_shape=out_shape, in_specs=[pl.BlockSpec(memory...]
where the time goes in v3:
time: 85.4 us; the launch traced here: 85.1 us
  Pallas kernels  81.4 us (95%)
  local copies, waits for them, and re-layouts  3.74 us (4%)
    pallas_call x1, Pallas kernels, call(): pl.pallas_call(kernel, out_shape=out_shape, in_specs=[pl.BlockSpec(memory...  81.4 us
    unnamed x2, local copies, waits for them, and re-layouts  3.74 us

profile of v3, /device:TPU:1, one launch (start us, length us, event | category | flops | bytes accessed | tf_op | source)
XLA Modules:
  0.0 85.1 jit_solution(14444517083392256455)
XLA Ops:
  0.0 1.9 %copy.12 = bf16[112,8,2,128]{3,1,2,0:T(8,128)(2,1)} copy(bf16[112,8,2,128]{3,2,1,0:T(2,128)(2,1)} %bitcast.12) | data formatting | bytes 917504
  1.9 81.4 %shard_map.91 = bf16[128,2048]{1,0:T(8,128)(2,1)} custom-call(s32[2,2]{1,0:T(2,128)} %nb_ref.1, bf16[8,2,64,896]{3,2,1,0:T(8,128)(2,1)} %bitcast.9, bf16[2,448,128]{2,1,0:T(8,128)(2,1)} %bitcast.13, bf16[448,896]{1,0:T(8,128)(2,1)} %bitcast.10, bf16[448,896]{1,0:T(8,128)(2,1)} %bitcast.11, bf16[896,256]{1,0:T(8,128)(2,1)} %bitcast.8, ...), custom_call_target="tpu_custom_call" | custom-call | tf_op jit(solution)/shard_map/pallas_call | solution.py:775
  83.3 1.9 %copy.14 = bf16[128,2048]{1,0:T(8,128)(2,1)} copy(bf16[128,2048]{1,0:T(8,128)(2,1)} %shard_map.91) | data formatting | bytes 1048576

commit v4 on v3

--- a/solution.py
+++ b/solution.py
@@ -290,7 +290,7 @@
 def span_kernel(
     n, spans, nb_ref, pas_in, mem_ref, wq_ref, wo_ref, kv_ref, ask_in, w_in, states_in, out_ref,
     enc, kvg, att_ref, w_all, states_ref, gathered, partial, crossed, summed, back,
-    pas_ref, ask_ref, nb_own, nbg, nbs, picks, got, swap, cop, mem, wq, wo, query, mixed,
+    kv_rows, kv_wide, pas_ref, ask_ref, nb_own, nbg, nbs, picks, got, swap, cop, mem, wq, wo, query, mixed,
     local_sem, nb_sem, pas_sem, swap_sem, w_sem, enc_sem, kvz_sem, kvy_sem, kvx_sem,
     wy_sem, wx_sem, att_sem, cross_sem, send_sem, back_sem,
 ):
@@ -317,6 +317,9 @@
 
     barrier, greeted = greet_all(n)
     pl.semaphore_signal(barrier, inc=1, device_id={"groups": twin}, device_id_type=MESH)
+    depth = kv_ref.shape[0] // 2
+    kv_load = pltpu.make_async_copy(kv_ref, kv_rows, local_sem.at[1])
+    kv_load.start()
     loads = [
         pltpu.make_async_copy(pas_in, pas_ref, local_sem.at[7]),
         pltpu.make_async_copy(ask_in, ask_ref, local_sem.at[8]),
@@ -327,6 +330,10 @@
         copy.start()
     nb_own[...] = jnp.zeros_like(nb_own)
     nb_own[:spans, :NB] = nb_ref[...]
+    kv_load.wait()
+    kv_wide[...] = kv_rows[...].astype(jnp.float32)
+    for i in range(2):
+        kvg[me, :, pl.ds(i * HD, HD)] = kv_wide[pl.ds(i, depth, stride=2)].astype(jnp.bfloat16)
     pl.semaphore_wait(barrier, greeted + 1)
 
     for d in range(1, n):
@@ -334,7 +341,6 @@
     own_nb = pltpu.make_async_copy(nb_own, nbg.at[me], local_sem.at[0])
     own_nb.start()
 
-    depth = kv_ref.shape[0]
     half, extra = depth // 2, depth // 56 * KV_EXTRA
     cut = (half + extra) // KV_CUTS
     parts = range(KV_CUTS)
@@ -351,22 +357,22 @@
 
     crossed_parts = [i for i in parts if i * cut < half - extra]
 
-    def along(source, travel, i, own, **how):
+    def along(source, travel, i, **how):
         lines = plane_part(i)
         spot = kvg.at[2 * source + y, lines]
         nxt = z + travel
         lane = (1 - travel) // 2
         copy = remote(
-            kv_ref.at[lines] if own else spot, spot, kvz_sem.at[0, source, lane, i], kvz_sem.at[1, source, lane, i],
+            spot, spot, kvz_sem.at[0, source, lane, i], kvz_sem.at[1, source, lane, i],
             span=2 * ((nxt + length) % length) + y,
         )
         go(copy, (nxt >= 0) & (nxt < length), **how)
 
-    def to_pair(source, i, own, **how):
+    def to_pair(source, i, **how):
         lines = plane_part(i)
         spot = kvg.at[2 * source + y, lines]
         go(remote(
-            kv_ref.at[lines] if own else spot, spot, kvy_sem.at[0, source, i], kvy_sem.at[1, source, i],
+            spot, spot, kvy_sem.at[0, source, i], kvy_sem.at[1, source, i],
             span=2 * z + 1 - y,
         ), **how)
 
@@ -385,8 +391,8 @@
                 remote(
                     spot, spot, kvz_sem.at[0, source, lane, i], kvz_sem.at[1, source, lane, i], span=2 * z + 1 - y,
                 ).wait_recv()
-            along(source, travel, i, False, start=start, note=note)
-            to_pair(source, i, False, start=start, note=note)
+            along(source, travel, i, start=start, note=note)
+            to_pair(source, i, start=start, note=note)
             to_twin(block, i, start=start, note=note)
 
     def pair_arrival(j):
@@ -404,8 +410,8 @@
 
     for i in parts:
         for travel in (1, -1):
-            along(z, travel, i, True)
-        to_pair(z, i, True)
+            along(z, travel, i)
+        to_pair(z, i)
 
     mine = pl.ds(pl.multiple_of(head * half_e, half_e), half_e)
     w_copies, own_copies = [], []
@@ -416,8 +422,6 @@
         w_copies[-1].start()
         own_copies.append(pltpu.make_async_copy(src, dst, local_sem.at[3 + i]))
         own_copies[-1].start()
-    own_copies.append(pltpu.make_async_copy(kv_ref, kvg.at[me], local_sem.at[1]))
-    own_copies[-1].start()
     own_nb.wait()
     loads[0].wait()
     for d in range(1, n):
@@ -871,9 +875,9 @@
         ]
         return call(
             functools.partial(span_kernel, n, span_count), 2, [states],
-            line_scratch + pas_scratch + [pltpu.VMEM(span_queries.shape, bf16)] + scratch + line_sems,
+            line_scratch + [pltpu.VMEM((2 * E, HD), bf16), pltpu.VMEM((2 * E, HD), jnp.float32)] + pas_scratch + [pltpu.VMEM(span_queries.shape, bf16)] + scratch + line_sems,
             [pltpu.VMEM] + [pl.ANY] * 8,
-            *operands, kv_weight.reshape(E, 2 * HD), span_queries, out_weight, span_states,
+            *operands, kv_weight.reshape(2 * E, HD), span_queries, out_weight, span_states,
             out_space=pl.ANY,
         )[0]
     kv = kv_weight.transpose(1, 0, 2)

time: 85.4 us -> 83.5 us (0.978)
  local copies, waits for them, and re-layouts: 3.74 us -> 1.88 us
    unnamed x2 -> x1, local copies, waits for them, and re-layouts: 3.74 us -> 1.88 us
where the time goes in v4:
time: 83.5 us; the launch traced here: 83.3 us
  Pallas kernels  81.4 us (97%)
  local copies, waits for them, and re-layouts  1.88 us (2%)
    pallas_call x1, Pallas kernels, call(): pl.pallas_call(kernel, out_shape=out_shape, in_specs=[pl.BlockSpec(memory...  81.4 us
    unnamed x1, local copies, waits for them, and re-layouts  1.88 us

profile of v4, /device:TPU:1, one launch (start us, length us, event | category | flops | bytes accessed | tf_op | source)
XLA Modules:
  0.0 83.3 jit_solution(10937799485896202450)
XLA Ops:
  0.0 81.4 %shard_map.91 = bf16[128,2048]{1,0:T(8,128)(2,1)} custom-call(s32[2,2]{1,0:T(2,128)} %nb_ref.1, bf16[8,2,64,896]{3,2,1,0:T(8,128)(2,1)} %bitcast.5, bf16[2,448,128]{2,1,0:T(8,128)(2,1)} %bitcast.9, bf16[448,896]{1,0:T(8,128)(2,1)} %bitcast.6, bf16[448,896]{1,0:T(8,128)(2,1)} %bitcast.7, bf16[1792,128]{1,0:T(8,128)(2,1)} %bitcast.8, ...), custom_call_target="tpu_custom_call" | custom-call | tf_op jit(solution)/shard_map/pallas_call | solution.py:779
  81.4 1.9 %copy.11 = bf16[128,2048]{1,0:T(8,128)(2,1)} copy(bf16[128,2048]{1,0:T(8,128)(2,1)} %shard_map.91) | data formatting | bytes 1048576

commit v5 on v4

--- a/solution.py
+++ b/solution.py
@@ -546,10 +546,14 @@
     for j in range(length):
         source = line_order(z, length, j)[0] if j else z
         blocks = [2 * source + y, 2 * source + 1 - y]
-        for block in blocks[0 if j else 1:]:
-            twin_arrival(block)
-        for block in blocks:
-            attend(block)
+        for k, block in enumerate(blocks):
+            if j or k:
+                twin_arrival(block)
+            if j == length - 1:
+                attend(block)
+        if j < length - 1:
+            for block in blocks:
+                attend(block)
         send_attended(source)
         if j == length - 1:
             for i in range(W_CROSS):

time: 83.5 us -> 83.2 us (level)
  no operation moved by 1% of the time
where the time goes in v5:
time: 83.2 us; the launch traced here: 83 us
  Pallas kernels  81.1 us (97%)
  local copies, waits for them, and re-layouts  1.88 us (2%)
    pallas_call x1, Pallas kernels, call(): pl.pallas_call(kernel, out_shape=out_shape, in_specs=[pl.BlockSpec(memory...  81.1 us
    unnamed x1, local copies, waits for them, and re-layouts  1.88 us

profile of v5, /device:TPU:1, one launch (start us, length us, event | category | flops | bytes accessed | tf_op | source)
XLA Modules:
  0.0 83.0 jit_solution(3841873037579321352)
XLA Ops:
  0.0 81.1 %shard_map.91 = bf16[128,2048]{1,0:T(8,128)(2,1)} custom-call(s32[2,2]{1,0:T(2,128)} %nb_ref.1, bf16[8,2,64,896]{3,2,1,0:T(8,128)(2,1)} %bitcast.5, bf16[2,448,128]{2,1,0:T(8,128)(2,1)} %bitcast.9, bf16[448,896]{1,0:T(8,128)(2,1)} %bitcast.6, bf16[448,896]{1,0:T(8,128)(2,1)} %bitcast.7, bf16[1792,128]{1,0:T(8,128)(2,1)} %bitcast.8, ...), custom_call_target="tpu_custom_call" | custom-call | tf_op jit(solution)/shard_map/pallas_call | solution.py:783
  81.1 1.9 %copy.11 = bf16[128,2048]{1,0:T(8,128)(2,1)} copy(bf16[128,2048]{1,0:T(8,128)(2,1)} %shard_map.91) | data formatting | bytes 1048576
